TPU v7x, 512 devices: a whole 4x4x16 slice. The times are simulated.
512 devices in a mesh: samp: 64 (over z, x), blk: 8 (over y, core).
Axes of the slice: x: 4, y: 4, z: 16, core: 2. Of those that a mesh axis runs over, the one named last changes fastest.
Arguments:
- genotypes: bfloat16 [65536, 4000], P('samp', 'blk'), may hold values from 0 to 2, as said below
- traits: float32 [65536, 8], P('samp'), may hold values from -3000 to 3000
- observed: int32 [65536, 8], P('samp'), may hold values from 0 to 1, as said below
- fold_index: int32 [65536], P('samp'), may hold values from 0 to 4, never falling along the last dimension, each value on 1 to 26214 neighbouring positions
Outputs:
- stack_gram: float32 [8, 5, 40, 40], P('blk')
- stack_cross: float32 [8, 5, 40], P('blk')
Inputs may be any that keep to these rules, and one draw needn't show every extreme that they name: `genotypes`: genotype dosages, whole numbers. `observed`: each trait is measured in at least one sample.
All inputs are finite; a program needn't handle non-finite values.
Results may differ from a plain program's by a relative error of at most 0.0003.
Values sent between devices are 32-bit elements; how exact they have to be, the bound alone decides.
A program may use at most 64 MiB of HBM per device.

v0:
```python
import jax
import jax.numpy as jnp
from jax import lax
from jax.sharding import PartitionSpec as P

BLOCK = 500
TRAITS = 8
FOLDS = 5
HERITABILITY = (0.01, 0.25, 0.5, 0.75, 0.99)
PRECISE = lax.Precision.HIGHEST


def solve_one(lower_factor, right_side):
    return jax.scipy.linalg.cho_solve((lower_factor, True), right_side)


def body(genotypes, traits, observed, fold_index):
    local_rows, local_cols = genotypes.shape
    local_blocks = local_cols // BLOCK
    sample_devices = lax.axis_size("samp")
    block_devices = lax.axis_size("blk")
    samples = local_rows * sample_devices
    markers = local_cols * block_devices
    penalty_count = len(HERITABILITY)
    present = observed.astype(jnp.float32)
    masked = present * traits
    dosage_bf = genotypes.reshape(local_rows, local_blocks, BLOCK)
    dosage = dosage_bf.astype(jnp.float32)
    gram_local = jnp.einsum(
        "sbi,sbj->bij", dosage_bf, dosage_bf, preferred_element_type=jnp.float32
    )
    sums_local = jnp.sum(dosage, 0)
    trait_local = jnp.einsum("sbj,sp->bjp", dosage, masked, precision=PRECISE)
    present_local = jnp.einsum("sbj,sp->bjp", dosage, present, precision=PRECISE)
    counts_local = jnp.sum(present, 0)
    first_local = jnp.sum(masked, 0)
    second_local = jnp.sum(masked * traits, 0)
    gram_total, column_sums, dosage_trait, dosage_present, counts, trait_sums, trait_squares = (
        lax.psum(
            (
                gram_local,
                sums_local,
                trait_local,
                present_local,
                counts_local,
                first_local,
                second_local,
            ),
            "samp",
        )
    )
    mean_trait = trait_sums / counts
    trait_scale = jnp.sqrt(trait_squares / counts - mean_trait * mean_trait + 1e-05)
    scaled = present * (traits - mean_trait) / trait_scale
    mean_dosage = column_sums / samples
    dosage_scale = jnp.sqrt(
        jnp.diagonal(gram_total, axis1=1, axis2=2) / samples - mean_dosage * mean_dosage + 1e-05
    )
    covariance = (gram_total - column_sums[:, :, None] * column_sums[:, None, :] / samples) / (
        dosage_scale[:, :, None] * dosage_scale[:, None, :]
    )
    right_side = (
        (dosage_trait - dosage_present * mean_trait) / trait_scale / dosage_scale[:, :, None]
    )
    identity = jnp.eye(BLOCK, dtype=jnp.float32)
    fit_count = local_blocks * penalty_count
    position = lax.axis_index("samp")
    assigned = jnp.minimum(
        (position * fit_count + sample_devices - 1) // sample_devices, fit_count - 1
    )
    owning = assigned * sample_devices // fit_count == position
    fit_block = assigned // penalty_count
    fit_penalty = assigned % penalty_count
    penalty_table = jnp.array(
        [markers * (1.0 - fraction) / fraction for fraction in HERITABILITY], dtype=jnp.float32
    )
    penalty = jnp.sum(jnp.where(jnp.arange(penalty_count) == fit_penalty, penalty_table, 0.0))
    chosen_cov = lax.dynamic_index_in_dim(covariance, fit_block, 0, keepdims=False)
    chosen_side = lax.dynamic_index_in_dim(right_side, fit_block, 0, keepdims=False)
    lower_factor = jnp.linalg.cholesky(chosen_cov + penalty * identity)
    solution = solve_one(lower_factor, chosen_side)
    selector = jnp.logical_and(jnp.arange(fit_count) == assigned, owning).astype(jnp.float32)
    contribution = selector[:, None, None] * solution[None]
    coefficients = lax.psum(contribution, "samp").reshape(
        local_blocks, penalty_count, BLOCK, TRAITS
    )
    centred = (dosage - mean_dosage) / dosage_scale
    predicted = jnp.einsum("sbj,brjp->pbrs", centred, coefficients, precision=PRECISE)
    energy = lax.psum(jnp.sum(predicted * predicted, 3), "samp")
    standard = predicted / jnp.sqrt(energy / samples + 1e-06)[:, :, :, None]
    regrouped = lax.all_to_all(standard, "blk", split_axis=0, concat_axis=1, tiled=True)
    trait_share = TRAITS // block_devices
    stacked = regrouped.reshape(trait_share, -1, local_rows)
    first_trait = lax.axis_index("blk") * trait_share
    scaled_share = lax.dynamic_slice_in_dim(scaled, first_trait, trait_share, 1)
    present_share = lax.dynamic_slice_in_dim(present, first_trait, trait_share, 1)
    fold_hits = (fold_index[None, :] == jnp.arange(FOLDS, dtype=jnp.int32)[:, None]).astype(
        jnp.float32
    )
    weighting = fold_hits[:, None, :] * present_share.T[None]
    weighted = weighting[:, :, None, :] * stacked[None]
    gram_part = jnp.einsum("kpls,pms->pklm", weighted, stacked, precision=PRECISE)
    cross_part = jnp.einsum("kpls,sp->pkl", weighted, scaled_share, precision=PRECISE)
    gram_sum, cross_sum = lax.psum((gram_part, cross_part), "samp")
    factor = FOLDS / samples
    return (gram_sum * factor, cross_sum * factor)


def solution(mesh):
    in_specs = (P("samp", "blk"), P("samp", None), P("samp", None), P("samp"))
    out_specs = (P("blk", None, None, None), P("blk", None, None))
    return jax.shard_map(body, mesh=mesh, in_specs=in_specs, out_specs=out_specs, check_vma=False)
```

profile of v0, /device:TPU:8, one launch (start us, length us, event | category | flops | bytes accessed | tf_op | source)
XLA Modules:
  0.0 1162.0 jit_solution(14717013578681250181)
XLA Ops:
  7.2 3.3 convolution_bitcast_fusion
  10.6 1.1 copy-done.1
  12.0 0.9 convolution_bitcast_fusion.1
  12.9 0.6 convert_element_type.18
  13.5 0.9 convolution_bitcast_fusion.2
  14.6 285.7 %all-reduce.4 = (f32[1,500]{1,0:T(1,128)S(1)}, f32[1,500,8]{1,2,0:T(8,128)}, f32[1,500,8]{1,2,0:T(8,128)}, f32[8]{0:T(128)S(1)}, f32[8]{0:T(128)S(1)}, /*index=5*/f32[8]{0:T(128)S(1)}) all-reduce(f32[1,500]{1,0:T(1,128)S(1)} %bitcast.135, f32[1,500,8]{1,2,0:T(8,128)S(1)} %convolution_bitcast_fusion.2, ...), channel_id=1, replica_groups=mesh['samp'=64,'blk'=8] {'samp'}, use_global_device_ids=true, to_apply=%region_2.0 | all-reduce | flops 8524 | bytes 68192 | tf_op jit(solution)/shard_map/psum | solution.py:39
  300.3 0.6 copy-done.11
  300.9 0.6 dynamic-slice.3
  301.4 0.6 dynamic-slice.4
  302.0 0.6 iota_multiply_fusion
  302.6 0.5 and_convert_fusion
  303.2 0.6 fusion.72
  303.8 10.4 gather_fusion
  314.2 0.6 broadcast_multiply_fusion.4
  314.8 1.9 bitcast_add_fusion.1
  316.7 1.5 copy.16
  318.3 1.0 fusion.14
  319.3 1.0 copy-done.2
  320.3 11.7 %cholesky.104 = f32[128,128]{1,0:T(8,128)S(1)} custom-call(f32[128,128]{1,0:T(8,128)S(1)} %cholesky.269), custom_call_target="Cholesky" | custom-call | tf_op jit(solution)/shard_map/jit(cholesky)/cholesky | solution.py:80
  332.1 0.6 select_reduce_fusion.2
  332.8 9.8 custom-call.34
  342.6 0.5 constant_dynamic-update-slice_fusion.3
  343.1 0.5 convolution_subtract_fusion
  343.6 0.6 cholesky.273
  344.2 13.2 %cholesky.217 = f32[128,128]{1,0:T(8,128)} custom-call(f32[128,128]{1,0:T(8,128)} %cholesky.273), custom_call_target="Cholesky" | custom-call | tf_op jit(solution)/shard_map/jit(cholesky)/cholesky | solution.py:80
  357.4 2.0 select_reduce_fusion.1
  359.4 11.4 custom-call.35
  370.8 1.2 convolution_dynamic-update-slice_fusion
  372.0 0.4 convolution_subtract_fusion.1
  372.4 12.3 %cholesky.238 = f32[128,128]{1,0:T(8,128)} custom-call(f32[128,128]{1,0:T(8,128)S(1)} %cholesky.278), custom_call_target="Cholesky" | custom-call | tf_op jit(solution)/shard_map/jit(cholesky)/cholesky | solution.py:80
  384.7 0.9 select_reduce_fusion
  385.6 0.7 compare_reduce_fusion.1
  386.3 10.4 custom-call.36
  396.8 1.1 convolution_dynamic-update-slice_fusion.1
  397.8 0.4 convolution_subtract_fusion.2
  398.2 10.8 cholesky.258
  409.1 0.6 compare_reduce_fusion
  409.7 1.3 compare_reduce_fusion.2
  413.8 0.5 copy-done.16
  414.2 6.3 while.1
  414.3 0.6 fusion.97
  414.9 1.4 bitcast_dynamic-update-slice_fusion.2
  416.4 0.6 fusion.97
  417.0 1.4 bitcast_dynamic-update-slice_fusion.2
  418.6 0.6 fusion.97
  419.2 1.4 bitcast_dynamic-update-slice_fusion.2
  420.7 39.3 %custom-call.37 = f32[4,128,128]{1,2,0:T(8,128)S(1)} custom-call(f32[4,128,128]{2,1,0:T(8,128)S(1)} %pad_maximum_fusion), custom_call_target="InvertDiagBlocksLowerTriangular" | custom-call | tf_op jit(solution)/shard_map/jit(_cho_solve)/triangular_solve | solution.py:14
  461.1 0.3 convolution_subtract_fusion.6
  462.2 0.2 convolution_subtract_fusion.4
  462.6 0.3 convolution_subtract_fusion.3
  463.2 0.7 broadcast_multiply_fusion.1
  463.9 0.8 constant_dynamic-slice_fusion.1
  464.7 257.0 %all-reduce.10.cloned.1.call-done = f32[5,500,8]{1,2,0:T(8,128)} async-done(((f32[5,500,8]{1,2,0:T(8,128)}), f32[5,500,8]{1,2,0:T(8,128)}) %all-reduce.10.cloned.1.call-update) | async-done | bytes 80016 | tf_op jit(solution)/shard_map/psum | solution.py:84
  721.7 2.5 multiply_reduce_fusion
  724.3 139.6 %psum.88 = f32[8,1,5]{2,0,1:T(8,128)S(1)} all-reduce(f32[8,1,5]{2,0,1:T(8,128)S(1)} %bitcast.133), channel_id=1, replica_groups=mesh['samp'=64,'blk'=8] {'samp'}, use_global_device_ids=true, to_apply=%region_22.23 | all-reduce | flops 40 | bytes 320 | tf_op jit(solution)/shard_map/psum | solution.py:89
  864.2 0.8 copy.19
  865.0 4.8 all-to-all-start
  869.8 5.0 all-to-all-done
  874.8 0.4 reduce.27
  875.3 3.2 fusion.4
  878.5 0.8 fusion.11
  879.3 274.3 %all-reduce.3 = (f32[1,5,40,40]{3,2,1,0:T(8,128)S(1)}, f32[1,5,40]{2,0,1:T(1,128)S(1)}) all-reduce(f32[1,5,40,40]{3,2,1,0:T(8,128)S(1)} %fusion.11, f32[1,5,40]{2,0,1:T(1,128)S(1)} %dot_general.44), channel_id=1, replica_groups=mesh['samp'=64,'blk'=8] {'samp'}, use_global_device_ids=true, to_apply=%region_23.24 | all-reduce | flops 8200 | bytes 65600 | tf_op jit(solution)/shard_map/psum | solution.py:104
  1153.7 0.7 broadcast_multiply_fusion
  1154.3 0.6 broadcast_multiply_fusion.2
  (77 shorter events, 3.8 us)
Async XLA Ops:
  7.2 296.6 %all-reduce.8.cloned.1.call-start = ((), (), s32[]{:S(2)}) async-start(), calls=%async_computation.1 | async-start | bytes 2064384 | tf_op jit(solution)/shard_map/psum | solution.py:39
  10.5 1.2 copy-start.1
  10.5 1.5 copy-start.4
  10.5 711.2 %all-reduce.10.cloned.1.call-start = ((), (), s32[]{:S(2)}) async-start(), calls=%async_computation.2 | async-start | bytes 163840 | tf_op jit(solution)/shard_map/psum | solution.py:84
  11.7 1.8 copy-start.5
  12.0 291.2 %copy-start.15 = (f32[5]{0:T(128)S(1)}, f32[5]{0:T(128)}, u32[]{:S(2)}) copy-start(f32[5]{0:T(128)} %constant.250.clone) | copy-start | bytes 64
  300.3 0.6 copy-start.11
  300.3 1.1 copy-start.9
  303.8 11.0 copy-start
  319.3 1.0 copy-start.2
  320.3 22.3 %copy-start.3 = (f32[500,500]{1,0:T(8,128)S(1)}, f32[500,500]{1,0:T(8,128)}, u32[]{:S(2)}) copy-start(f32[500,500]{1,0:T(8,128)} %copy-done.2) | copy-start | bytes 3000004
  413.6 0.7 copy-start.16
  413.7 46.3 %copy-start.6 = (f32[1,500,8]{1,2,0:T(8,128)S(1)}, f32[1,500,8]{1,2,0:T(8,128)}, u32[]{:S(2)}) copy-start(f32[1,500,8]{1,2,0:T(8,128)} %get-tuple-element.24) | copy-start | bytes 48004
  413.7 46.3 %copy-start.7 = (f32[1,500,8]{1,2,0:T(8,128)S(1)}, f32[1,500,8]{1,2,0:T(8,128)}, u32[]{:S(2)}) copy-start(f32[1,500,8]{1,2,0:T(8,128)} %get-tuple-element.25) | copy-start | bytes 48004
  413.7 46.3 %copy-start.10 = (f32[8]{0:T(128)S(1)}, f32[8]{0:T(128)}, u32[]{:S(2)}) copy-start(f32[8]{0:T(128)} %copy-done.9) | copy-start | bytes 100
  413.7 46.3 %copy-start.12 = (f32[8]{0:T(128)S(1)}, f32[8]{0:T(128)}, u32[]{:S(2)}) copy-start(f32[8]{0:T(128)} %copy-done.11) | copy-start | bytes 100
  420.7 42.5 %copy-start.14 = (f32[5]{0:T(128)S(1)}, f32[5]{0:T(128)}, u32[]{:S(2)}) copy-start(f32[5]{0:T(128)} %and_convert_fusion) | copy-start | bytes 64
  420.7 301.0 %copy-start.13 = (f32[1,500]{1,0:T(1,128)S(1)}, f32[1,500]{1,0:T(1,128)}, u32[]{:S(2)}) copy-start(f32[1,500]{1,0:T(1,128)} %get-tuple-element.43) | copy-start | bytes 6004
  721.7 148.1 %copy-start.8 = (s32[1024]{0:T(1024)S(1)}, s32[1024]{0:T(1024)}, u32[]{:S(2)}) copy-start(s32[1024]{0:T(1024)} %param.8) | copy-start | bytes 12292
  865.0 9.8 all-to-all-start
Sparse Core Ops, SparseCore 0:
  11.4 280.3 all-reduce.7
  464.0 257.6 all-reduce.9
where the time goes:
time: 1170 us; the launch traced here: 1160 us
  blocking collectives  700 us (60%)
  waiting for transfers between devices  262 us (22%)
  other arithmetic  134 us (11%)
  local copies, waits for them, and re-layouts  25.2 us (2%)
  matrix products  18.5 us (2%)
  between operations  17.3 us (1%)
    psum x1, blocking collectives, body(): lax.psum((gram_local, sums_local, trait_local, present_local, counts_loca...  286 us
    psum x1, blocking collectives, body(): gram_sum, cross_sum = lax.psum((gram_part, cross_part), 'samp')  274 us
    psum x1, waiting for transfers between devices, body(): lax.psum(contribution, 'samp')  257 us
    psum x1, blocking collectives, body(): energy = lax.psum(jnp.sum(predicted * predicted, 3), 'samp')  140 us
    another operation x14, other arithmetic, body(): lower_factor = jnp.linalg.cholesky(chosen_cov + penalty * identity)  85.9 us
    another operation x8, other arithmetic, solve_one(): return jax.scipy.linalg.cho_solve((lower_factor, True), right_side)  40.2 us
  transfers between devices with their start and end apart: 3, of which 2 were waited for; matrix products, arithmetic and copies ran while one was open for 1% of the time, Pallas kernels for 0%

commit v1 on v0

--- a/solution.py
+++ b/solution.py
@@ -86,7 +86,7 @@
     )
     centred = (dosage - mean_dosage) / dosage_scale
     predicted = jnp.einsum("sbj,brjp->pbrs", centred, coefficients, precision=PRECISE)
-    energy = lax.psum(jnp.sum(predicted * predicted, 3), "samp")
+    energy = jnp.sum(lax.all_gather(jnp.sum(predicted * predicted, 3), "samp"), axis=0)
     standard = predicted / jnp.sqrt(energy / samples + 1e-06)[:, :, :, None]
     regrouped = lax.all_to_all(standard, "blk", split_axis=0, concat_axis=1, tiled=True)
     trait_share = TRAITS // block_devices

time: 1170 us -> 1110 us (0.949)
  blocking collectives: 700 us -> 643 us
    psum x1 -> x0, blocking collectives: 140 us -> none  [body(): energy = lax.psum(jnp.sum(predicted * predicted, 3), 'samp')]
    all_gather x0 -> x1, blocking collectives: none -> 80.5 us  [body(): lax.all_gather(jnp.sum(predicted * predicted, 3), 'samp')]
where the time goes in v1:
time: 1110 us
  blocking collectives  643 us (58%)
  waiting for transfers between devices  262 us (24%)
  other arithmetic  134 us (12%)
  local copies, waits for them, and re-layouts  25.2 us (2%)
  matrix products  18.5 us (2%)
  between operations  17.3 us (2%)
    psum x1, blocking collectives, body(): lax.psum((gram_local, sums_local, trait_local, present_local, counts_loca...  286 us
    psum x1, blocking collectives, body(): gram_sum, cross_sum = lax.psum((gram_part, cross_part), 'samp')  277 us
    psum x1, waiting for transfers between devices, body(): lax.psum(contribution, 'samp')  257 us
    another operation x14, other arithmetic, body(): lower_factor = jnp.linalg.cholesky(chosen_cov + penalty * identity)  85.9 us
    all_gather x1, blocking collectives, body(): lax.all_gather(jnp.sum(predicted * predicted, 3), 'samp')  80.5 us
    another operation x8, other arithmetic, solve_one(): return jax.scipy.linalg.cho_solve((lower_factor, True), right_side)  40.2 us
  transfers between devices with their start and end apart: 3, of which 2 were waited for; matrix products, arithmetic and copies ran while one was open for 1% of the time, Pallas kernels for 0%

profile of v1, /device:TPU:8, one launch (start us, length us, event | category | flops | bytes accessed | tf_op | source)
XLA Modules:
  0.0 1105.2 jit_solution(12713014126597593145)
XLA Ops:
  7.2 3.3 convolution_bitcast_fusion
  10.6 1.1 copy-done.1
  12.0 0.9 convolution_bitcast_fusion.1
  12.9 0.6 convert_element_type.18
  13.5 0.9 convolution_bitcast_fusion.2
  14.6 285.7 %all-reduce.4 = (f32[1,500]{1,0:T(1,128)S(1)}, f32[1,500,8]{1,2,0:T(8,128)}, f32[1,500,8]{1,2,0:T(8,128)}, f32[8]{0:T(128)S(1)}, f32[8]{0:T(128)S(1)}, /*index=5*/f32[8]{0:T(128)S(1)}) all-reduce(f32[1,500]{1,0:T(1,128)S(1)} %bitcast.133, f32[1,500,8]{1,2,0:T(8,128)S(1)} %convolution_bitcast_fusion.2, ...), channel_id=1, replica_groups=mesh['samp'=64,'blk'=8] {'samp'}, use_global_device_ids=true, to_apply=%region_2.0 | all-reduce | flops 8524 | bytes 68192 | tf_op jit(solution)/shard_map/psum | solution.py:39
  300.3 0.6 copy-done.11
  300.9 0.6 dynamic-slice.3
  301.4 0.6 dynamic-slice.4
  302.0 0.6 iota_multiply_fusion
  302.6 0.5 and_convert_fusion
  303.2 0.6 fusion.72
  303.8 10.4 gather_fusion
  314.2 0.6 broadcast_multiply_fusion.4
  314.8 1.9 bitcast_add_fusion.1
  316.7 1.5 copy.14
  318.3 1.0 fusion.14
  319.3 1.0 copy-done.2
  320.3 11.7 %cholesky.104 = f32[128,128]{1,0:T(8,128)S(1)} custom-call(f32[128,128]{1,0:T(8,128)S(1)} %cholesky.269), custom_call_target="Cholesky" | custom-call | tf_op jit(solution)/shard_map/jit(cholesky)/cholesky | solution.py:80
  332.1 0.6 select_reduce_fusion.2
  332.8 9.8 custom-call.34
  342.6 0.5 constant_dynamic-update-slice_fusion.3
  343.1 0.5 convolution_subtract_fusion
  343.6 0.6 cholesky.273
  344.2 13.2 %cholesky.217 = f32[128,128]{1,0:T(8,128)} custom-call(f32[128,128]{1,0:T(8,128)} %cholesky.273), custom_call_target="Cholesky" | custom-call | tf_op jit(solution)/shard_map/jit(cholesky)/cholesky | solution.py:80
  357.4 2.0 select_reduce_fusion.1
  359.4 11.4 %custom-call.35 = f32[1,128,128]{1,2,0:T(8,128)} custom-call(f32[1,128,128]{2,1,0:T(8,128)} %get-tuple-element.37), custom_call_target="InvertDiagBlocksLowerTriangular" | custom-call | tf_op jit(solution)/shard_map/jit(cholesky)/cholesky | solution.py:80
  370.8 1.2 convolution_dynamic-update-slice_fusion
  372.0 0.4 convolution_subtract_fusion.1
  372.4 12.3 %cholesky.238 = f32[128,128]{1,0:T(8,128)} custom-call(f32[128,128]{1,0:T(8,128)S(1)} %cholesky.278), custom_call_target="Cholesky" | custom-call | tf_op jit(solution)/shard_map/jit(cholesky)/cholesky | solution.py:80
  384.7 0.9 select_reduce_fusion
  385.6 0.7 compare_reduce_fusion.1
  386.3 10.4 custom-call.36
  396.8 1.1 convolution_dynamic-update-slice_fusion.1
  397.8 0.4 convolution_subtract_fusion.2
  398.2 10.8 cholesky.258
  409.1 0.6 compare_reduce_fusion
  409.7 1.3 compare_reduce_fusion.2
  413.8 0.5 copy-done.16
  414.2 6.3 while.1
  414.3 0.6 fusion.97
  414.9 1.4 bitcast_dynamic-update-slice_fusion.2
  416.4 0.6 fusion.97
  417.0 1.4 bitcast_dynamic-update-slice_fusion.2
  418.6 0.6 fusion.97
  419.2 1.4 bitcast_dynamic-update-slice_fusion.2
  420.7 39.3 %custom-call.37 = f32[4,128,128]{1,2,0:T(8,128)S(1)} custom-call(f32[4,128,128]{2,1,0:T(8,128)S(1)} %pad_maximum_fusion), custom_call_target="InvertDiagBlocksLowerTriangular" | custom-call | tf_op jit(solution)/shard_map/jit(_cho_solve)/triangular_solve | solution.py:14
  461.1 0.3 convolution_subtract_fusion.6
  462.2 0.2 convolution_subtract_fusion.4
  462.6 0.3 convolution_subtract_fusion.3
  463.2 0.7 broadcast_multiply_fusion.1
  463.9 0.8 constant_dynamic-slice_fusion.1
  464.7 257.0 %all-reduce.10.cloned.1.call-done = f32[5,500,8]{1,2,0:T(8,128)} async-done(((f32[5,500,8]{1,2,0:T(8,128)}), f32[5,500,8]{1,2,0:T(8,128)}) %all-reduce.10.cloned.1.call-update) | async-done | bytes 80016 | tf_op jit(solution)/shard_map/psum | solution.py:84
  721.7 2.5 multiply_reduce_fusion
  724.3 80.5 %all-gather = f32[512,5]{1,0:T(8,128)S(1)} all-gather(f32[8,5]{1,0:T(8,128)S(1)} %copy.15), channel_id=2, replica_groups=mesh['samp'=64,'blk'=8] {'samp'}, dimensions={0}, use_global_device_ids=true | all-gather | bytes 10400 | tf_op jit(solution)/shard_map/all_gather | solution.py:89
  805.1 0.8 copy.17
  806.0 4.8 all-to-all-start
  810.8 5.0 all-to-all-done
  815.8 0.4 reduce.29
  816.2 3.2 fusion.4
  819.5 0.8 fusion.11
  820.3 276.6 %all-reduce.3 = (f32[1,5,40,40]{3,2,1,0:T(8,128)S(1)}, f32[1,5,40]{2,0,1:T(1,128)S(1)}) all-reduce(f32[1,5,40,40]{3,2,1,0:T(8,128)S(1)} %fusion.11, f32[1,5,40]{2,0,1:T(1,128)S(1)} %dot_general.44), channel_id=1, replica_groups=mesh['samp'=64,'blk'=8] {'samp'}, use_global_device_ids=true, to_apply=%region_23.24 | all-reduce | flops 8200 | bytes 65600 | tf_op jit(solution)/shard_map/psum | solution.py:104
  1096.9 0.7 broadcast_multiply_fusion
  1097.6 0.6 broadcast_multiply_fusion.2
  (78 shorter events, 3.9 us)
Async XLA Ops:
  7.2 296.6 %all-reduce.8.cloned.1.call-start = ((), (), s32[]{:S(2)}) async-start(), calls=%async_computation.1 | async-start | bytes 2064384 | tf_op jit(solution)/shard_map/psum | solution.py:39
  10.5 1.2 copy-start.1
  10.5 1.5 copy-start.4
  10.5 711.2 %all-reduce.10.cloned.1.call-start = ((), (), s32[]{:S(2)}) async-start(), calls=%async_computation.2 | async-start | bytes 163840 | tf_op jit(solution)/shard_map/psum | solution.py:84
  11.7 1.8 copy-start.5
  12.0 291.2 %copy-start.15 = (f32[5]{0:T(128)S(1)}, f32[5]{0:T(128)}, u32[]{:S(2)}) copy-start(f32[5]{0:T(128)} %constant.250.clone) | copy-start | bytes 64
  300.3 0.6 copy-start.11
  300.3 1.1 copy-start.9
  303.8 11.0 copy-start
  319.3 1.0 copy-start.2
  320.3 22.3 %copy-start.3 = (f32[500,500]{1,0:T(8,128)S(1)}, f32[500,500]{1,0:T(8,128)}, u32[]{:S(2)}) copy-start(f32[500,500]{1,0:T(8,128)} %copy-done.2) | copy-start | bytes 3000004
  413.6 0.7 copy-start.16
  413.7 46.3 %copy-start.6 = (f32[1,500,8]{1,2,0:T(8,128)S(1)}, f32[1,500,8]{1,2,0:T(8,128)}, u32[]{:S(2)}) copy-start(f32[1,500,8]{1,2,0:T(8,128)} %get-tuple-element.24) | copy-start | bytes 48004
  413.7 46.3 %copy-start.7 = (f32[1,500,8]{1,2,0:T(8,128)S(1)}, f32[1,500,8]{1,2,0:T(8,128)}, u32[]{:S(2)}) copy-start(f32[1,500,8]{1,2,0:T(8,128)} %get-tuple-element.25) | copy-start | bytes 48004
  413.7 46.3 %copy-start.10 = (f32[8]{0:T(128)S(1)}, f32[8]{0:T(128)}, u32[]{:S(2)}) copy-start(f32[8]{0:T(128)} %copy-done.9) | copy-start | bytes 100
  413.7 46.3 %copy-start.12 = (f32[8]{0:T(128)S(1)}, f32[8]{0:T(128)}, u32[]{:S(2)}) copy-start(f32[8]{0:T(128)} %copy-done.11) | copy-start | bytes 100
  420.7 42.5 %copy-start.14 = (f32[5]{0:T(128)S(1)}, f32[5]{0:T(128)}, u32[]{:S(2)}) copy-start(f32[5]{0:T(128)} %and_convert_fusion) | copy-start | bytes 64
  420.7 301.0 %copy-start.13 = (f32[1,500]{1,0:T(1,128)S(1)}, f32[1,500]{1,0:T(1,128)}, u32[]{:S(2)}) copy-start(f32[1,500]{1,0:T(1,128)} %get-tuple-element.43) | copy-start | bytes 6004
  724.2 86.5 %copy-start.8 = (s32[1024]{0:T(1024)S(1)}, s32[1024]{0:T(1024)}, u32[]{:S(2)}) copy-start(s32[1024]{0:T(1024)} %param.8) | copy-start | bytes 12292
  806.0 9.8 all-to-all-start
Sparse Core Ops, SparseCore 0:
  11.4 280.3 all-reduce.7
  464.0 257.6 all-reduce.9
